TPU v7x, 32 devices: a whole 2x2x4 slice. The times are simulated.
32 devices in a mesh: fsdp: 4 (over y, core), ctx: 8 (over z, x).
Axes of the slice: x: 2, y: 2, z: 4, core: 2. Of those that a mesh axis runs over, the one named last changes fastest.
Arguments:
- query_proj: bfloat16 [4, 1024, 4096], P('fsdp', 'ctx'), may hold values from -10 to 10
- key_proj: bfloat16 [4, 1024, 4096], P('fsdp', 'ctx'), may hold values from -10 to 10
- value_proj: bfloat16 [4, 1024, 4096], P('fsdp', 'ctx'), may hold values from -12 to 12
- modality: int32 [4, 1024], P('fsdp', 'ctx'), may hold values from 0 to 1, as said below
- out_weight: bfloat16 [2, 4096, 2048], P(None, ('fsdp', 'ctx')), may hold values from -0.09375 to 0.09375
- grad_projected: bfloat16 [4, 1024, 2048], P('fsdp', 'ctx'), may hold values from -6 to 6
Outputs:
- projected: bfloat16 [4, 1024, 2048], P('fsdp', 'ctx')
- grad_query: bfloat16 [4, 1024, 4096], P('fsdp', 'ctx')
- grad_key: bfloat16 [4, 1024, 4096], P('fsdp', 'ctx')
- grad_value: bfloat16 [4, 1024, 4096], P('fsdp', 'ctx')
Inputs may be any that keep to these rules, and one draw needn't show every extreme that they name: `modality`: each sequence holds exactly two image spans of 256 positions each, one starting within the first half and lying in the first half, the other lying in the second half; all other positions are text, so exactly half of each sequence's positions are image.
All inputs are finite; a program needn't handle non-finite values.
Results may differ from a plain program's by a relative error of at most 0.012.
The roundings to bfloat16 on the way count: a program that leaves them out, or rounds other values in their place, can miss the bound.
Values may be sent and summed in bfloat16 or wider, within the bound.
A program may use at most 320 MiB of HBM per device.

v0:
```python
import jax
import jax.numpy as jnp
from jax import lax
from jax.sharding import PartitionSpec as P

HEAD_SIZE = 128


def block_count(length):
    return max(1, min(8, length // 512))


def probabilities(query_block, key_prefix, offset):
    scaling = query_block.shape[-1] ** (-0.5)
    scores = (
        jnp.einsum("hqd,hkd->hqk", query_block, key_prefix, preferred_element_type=jnp.float32)
        * scaling
    )
    query_places = offset + jnp.arange(query_block.shape[1])
    key_places = jnp.arange(key_prefix.shape[1])
    scores = jnp.where(key_places[None, None, :] <= query_places[None, :, None], scores, -jnp.inf)
    highest = jnp.max(scores, axis=-1, keepdims=True)
    raised = jnp.exp(scores - highest)
    return raised / jnp.sum(raised, axis=-1, keepdims=True)


def attend_forward(queries, keys_all, values_all):
    length = queries.shape[1]
    block_rows = length // block_count(length)
    pieces = []
    for block_index in range(length // block_rows):
        offset = block_index * block_rows
        finish = offset + block_rows
        weights = probabilities(queries[:, offset:finish], keys_all[:, :finish], offset).astype(
            jnp.bfloat16
        )
        output = jnp.einsum(
            "hqk,hkd->hqd", weights, values_all[:, :finish], preferred_element_type=jnp.float32
        )
        pieces.append(output.astype(jnp.bfloat16))
    return jnp.concatenate(pieces, axis=1)


def attend_backward(queries, keys_all, values_all, attention, grad_attention):
    length = queries.shape[1]
    block_rows = length // block_count(length)
    scaling = queries.shape[-1] ** (-0.5)
    grad_keys = jnp.zeros(queries.shape, jnp.float32)
    grad_values = jnp.zeros(queries.shape, jnp.float32)
    query_pieces = []
    for block_index in range(length // block_rows):
        offset = block_index * block_rows
        finish = offset + block_rows
        query_block = queries[:, offset:finish]
        weights = probabilities(query_block, keys_all[:, :finish], offset)
        grad_block = grad_attention[:, offset:finish]
        attn_block = attention[:, offset:finish]
        grad_values = grad_values.at[:, :finish].add(
            jnp.einsum(
                "hqk,hqd->hkd",
                weights.astype(jnp.bfloat16),
                grad_block,
                preferred_element_type=jnp.float32,
            )
        )
        grad_weights = jnp.einsum(
            "hqd,hkd->hqk", grad_block, values_all[:, :finish], preferred_element_type=jnp.float32
        )
        row_delta = jnp.sum(
            grad_block.astype(jnp.float32) * attn_block.astype(jnp.float32), axis=-1, keepdims=True
        )
        grad_scores = (weights * (grad_weights - row_delta) * scaling).astype(jnp.bfloat16)
        query_pieces.append(
            jnp.einsum(
                "hqk,hkd->hqd",
                grad_scores,
                keys_all[:, :finish],
                preferred_element_type=jnp.float32,
            ).astype(jnp.bfloat16)
        )
        grad_keys = grad_keys.at[:, :finish].add(
            jnp.einsum("hqk,hqd->hkd", grad_scores, query_block, preferred_element_type=jnp.float32)
        )
    return (
        jnp.concatenate(query_pieces, axis=1),
        grad_keys.astype(jnp.bfloat16),
        grad_values.astype(jnp.bfloat16),
    )


def transposed_product(left, right):
    return lax.dot_general(
        left, right, (((1,), (1,)), ((), ())), preferred_element_type=jnp.float32
    )


def heads_first(flat, length, local_heads):
    return flat.reshape(length, local_heads, HEAD_SIZE).transpose(1, 0, 2)


def heads_last(stacked, length, local_width):
    return stacked.transpose(1, 0, 2).reshape(1, length, local_width)


def per_device(query_proj, key_proj, value_proj, modality, out_weight, grad_projected):
    context_size = lax.axis_size("ctx")
    row_count = query_proj.shape[1]
    inner_width = query_proj.shape[2]
    length = row_count * context_size
    local_width = inner_width // context_size
    local_heads = local_width // HEAD_SIZE
    head_query, head_key, head_value = (
        lax.all_to_all(query_proj, "ctx", split_axis=2, concat_axis=1, tiled=True),
        lax.all_to_all(key_proj, "ctx", split_axis=2, concat_axis=1, tiled=True),
        lax.all_to_all(value_proj, "ctx", split_axis=2, concat_axis=1, tiled=True),
    )
    head_query = heads_first(head_query, length, local_heads)
    head_key = heads_first(head_key, length, local_heads)
    head_value = heads_first(head_value, length, local_heads)
    attention = attend_forward(head_query, head_key, head_value)
    sending = heads_last(attention, length, local_width)
    attn_rows = lax.all_to_all(sending, "ctx", split_axis=1, concat_axis=2, tiled=True)[0]
    upstream = grad_projected[0]
    weight_piece = lax.all_gather(out_weight, ("fsdp", "ctx"), axis=1, tiled=True)
    text_out = jnp.dot(attn_rows, weight_piece[0], preferred_element_type=jnp.float32)
    image_out = jnp.dot(attn_rows, weight_piece[1], preferred_element_type=jnp.float32)
    text_grad = transposed_product(upstream, weight_piece[0])
    image_grad = transposed_product(upstream, weight_piece[1])
    text_out, image_out, text_grad, image_grad = (text_out, image_out, text_grad, image_grad)
    image_rows = (modality[0] == 1)[:, None]
    projected = jnp.where(image_rows, image_out, text_out).astype(jnp.bfloat16)[None]
    grad_rows = jnp.where(image_rows, image_grad, text_grad).astype(jnp.bfloat16)
    grad_heads = lax.all_to_all(grad_rows[None], "ctx", split_axis=2, concat_axis=1, tiled=True)
    grad_heads = heads_first(grad_heads, length, local_heads)
    grad_q, grad_k, grad_v = attend_backward(
        head_query, head_key, head_value, attention, grad_heads
    )
    grad_query, grad_key, grad_value = (
        lax.all_to_all(
            heads_last(grad_q, length, local_width), "ctx", split_axis=1, concat_axis=2, tiled=True
        ),
        lax.all_to_all(
            heads_last(grad_k, length, local_width), "ctx", split_axis=1, concat_axis=2, tiled=True
        ),
        lax.all_to_all(
            heads_last(grad_v, length, local_width), "ctx", split_axis=1, concat_axis=2, tiled=True
        ),
    )
    return (projected, grad_query, grad_key, grad_value)


def solution(mesh):
    placed = (
        P("fsdp", "ctx", None),
        P("fsdp", "ctx", None),
        P("fsdp", "ctx", None),
        P("fsdp", "ctx"),
        P(None, ("fsdp", "ctx"), None),
        P("fsdp", "ctx", None),
    )
    return jax.shard_map(
        per_device,
        mesh=mesh,
        in_specs=placed,
        out_specs=(
            P("fsdp", "ctx", None),
            P("fsdp", "ctx", None),
            P("fsdp", "ctx", None),
            P("fsdp", "ctx", None),
        ),
        check_vma=False,
    )
```

profile of v0, /device:TPU:0, one launch (start us, length us, event | category | flops | bytes accessed | tf_op | source)
XLA Modules:
  0.0 543.5 jit_solution(6970841541703421704)
XLA Ops:
  7.9 5.0 copy.130
  13.5 23.4 %reduce.8 = bf16[4096,128]{1,0:T(8,128)(2,1)} reduce(bf16[4096,1,128]{2,1,0:T(2,128)(2,1)S(1)} %bitcast.141, bf16[]{:T(256)} %broadcast.182), dimensions={1}, to_apply=%bitcast.103.reduce_sub_computation | reduce | bytes 2097154
  36.8 2.1 reshape.224
  39.0 7.3 %all-to-all-start = ((bf16[8,2,32768]{2,1,0:T(2,128)(2,1)}), bf16[8,2,32768]{2,1,0:T(2,128)(2,1)}, u32[]{:S(2)}, u32[]{:S(2)}) async-start(bf16[8,2,32768]{2,1,0:T(2,128)(2,1)} %reshape.224), calls=%async_computation | async-start | bytes 2097152 | tf_op jit(solution)/shard_map/all_to_all | solution.py:113
  46.2 5.0 copy.133
  51.3 23.4 %reduce.9 = bf16[4096,128]{1,0:T(8,128)(2,1)} reduce(bf16[4096,1,128]{2,1,0:T(2,128)(2,1)S(1)} %bitcast.147, bf16[]{:T(256)} %broadcast.182), dimensions={1}, to_apply=%bitcast.105.reduce_sub_computation | reduce | bytes 2097154
  74.6 2.1 reshape.226
  76.8 16.4 %all-to-all-done = bf16[8,2,32768]{2,1,0:T(2,128)(2,1)} async-done(((bf16[8,2,32768]{2,1,0:T(2,128)(2,1)}), bf16[8,2,32768]{2,1,0:T(2,128)(2,1)}, u32[]{:S(2)}, u32[]{:S(2)}) %all-to-all-start) | async-done | bytes 1048608 | tf_op jit(solution)/shard_map/all_to_all | solution.py:113
  93.2 7.5 %all-to-all-start.1 = ((bf16[8,2,32768]{2,1,0:T(2,128)(2,1)}), bf16[8,2,32768]{2,1,0:T(2,128)(2,1)}, u32[]{:S(2)}, u32[]{:S(2)}) async-start(bf16[8,2,32768]{2,1,0:T(2,128)(2,1)} %reshape.226), calls=%async_computation.1 | async-start | bytes 2097152 | tf_op jit(solution)/shard_map/all_to_all | solution.py:114
  100.7 5.0 copy.136
  105.7 23.4 %reduce.10 = bf16[4096,128]{1,0:T(8,128)(2,1)} reduce(bf16[4096,1,128]{2,1,0:T(2,128)(2,1)S(1)} %bitcast.148, bf16[]{:T(256)} %broadcast.182), dimensions={1}, to_apply=%bitcast.107.reduce_sub_computation | reduce | bytes 2097154
  129.1 2.1 reshape.228
  131.7 4.3 reshape.225
  139.9 5.2 all-to-all-start.2
  145.1 4.4 reshape.227
  153.3 5.2 fusion.58
  158.5 103.3 %all-gather.2.cloned.1.call-done = bf16[2,4096,2048]{2,1,0:T(8,128)(2,1)} async-done(((bf16[2,128,2048]{2,1,0:T(8,128)(2,1)}), bf16[2,4096,2048]{2,1,0:T(8,128)(2,1)}) %all-gather.2.cloned.1.call-update) | async-done | bytes 33554448 | tf_op jit(solution)/shard_map/all_gather | solution.py:124
  261.9 11.4 %fusion.2 = bf16[128,4096]{1,0:T(8,128)(2,1)S(1)} fusion(bf16[2,4096,2048]{2,1,0:T(8,128)(2,1)} %all-gather.2.cloned.1.call-done, bf16[1,128,2048]{2,1,0:T(8,128)(2,1)S(1)} %copy-done), kind=kOutput, calls=%fused_computation.4 | convolution fusion | flops 2147483648 | bytes 18350080 | tf_op jit(solution)/shard_map/dot_general | solution.py:92
  273.2 12.3 %fusion.9 = bf16[1,128,4096]{2,1,0:T(8,128)(2,1)} fusion(bf16[128,4096]{1,0:T(8,128)(2,1)S(1)} %fusion.2, bf16[2,4096,2048]{2,1,0:T(8,128)(2,1)} %all-gather.2.cloned.1.call-done, pred[128]{0:T(512)(128)(4,1)S(1)} %compare_bitcast_fusion, bf16[1,128,2048]{2,1,0:T(8,128)(2,1)S(1)} %copy-done), kind=kOutput, calls=%fused_computation.14 | convolution fusion | flops 2148007936 | bytes 19398784 | tf_op jit(solution)/shard_map/dot_general | solution.py:92
  285.6 5.0 copy.143
  290.6 23.5 %reduce.11 = bf16[4096,128]{1,0:T(8,128)(2,1)} reduce(bf16[4096,1,128]{2,1,0:T(2,128)(2,1)S(1)} %bitcast.143, bf16[]{:T(256)} %broadcast.182), dimensions={1}, to_apply=%bitcast.111.reduce_sub_computation | reduce | bytes 2097154
  314.2 2.1 reshape.232
  316.3 4.2 all-to-all-start.4
  320.6 5.3 fusion.13
  325.9 4.3 reshape.229
  332.0 2.3 reshape.218
  334.3 2.3 copy.138
  340.3 2.1 fusion.67
  345.1 2.0 all-to-all-done.4
  347.0 5.8 %reshape.233 = bf16[4096,1,128]{2,1,0:T(2,128)(2,1)} reshape(bf16[8,2,32768]{2,1,0:T(2,128)(2,1)} %all-to-all-done.4) | data formatting | bytes 2097152
  356.2 2.3 reshape.220
  358.5 2.3 copy.145
  360.7 2.7 multiply_reduce_fusion.1
  363.5 2.0 multiply_convert_fusion.1
  366.6 2.3 copy.140
  368.9 6.1 %copy.141 = bf16[1,1024,512]{2,0,1:T(2,128)(2,1)} copy(bf16[1,1024,512]{1,2,0:T(8,128)(2,1)} %bitcast.157) | data formatting | bytes 2097152 | tf_op jit(solution)/shard_map/reshape | solution.py:102
  375.0 9.0 %reduce.12 = bf16[1024,512]{1,0:T(8,128)(2,1)} reduce(bf16[1024,1,512]{2,1,0:T(2,128)(2,1)} %bitcast.144, bf16[]{:T(256)} %broadcast.182), dimensions={1}, to_apply=%bitcast.109.reduce_sub_computation | reduce | bytes 2097154
  384.1 2.6 reshape.230
  386.7 4.6 all-to-all-start.3
  393.2 5.5 %multiply_convert_fusion = bf16[4,512,1024]{2,1,0:T(8,128)(2,1)S(1)} fusion(f32[4,512]{1,0:T(4,128)S(1)} %get-tuple-element.85, f32[4,512,1024]{2,1,0:T(8,128)} %get-tuple-element.87, f32[4,512]{1,0:T(4,128)S(1)} %get-tuple-element.86, bf16[4,1024,128]{2,1,0:T(8,128)(2,1)} %bitcast.172, bf16[1024,4,128]{2,0,1:T(8,128)(2,1)} %copy.138), kind=kOutput, calls=%fused_computation.8 | convolution fusion | flops 547356672 | bytes 14172160 | tf_op jit(solution)/shard_map/hqd,hkd->hqk/dot_general | solution.py:66
  398.7 2.2 add_convert_fusion.1
  401.0 6.0 %copy.154 = bf16[1,1024,512]{2,0,1:T(2,128)(2,1)} copy(bf16[1,1024,512]{1,2,0:T(8,128)(2,1)} %bitcast.166) | data formatting | bytes 2097152 | tf_op jit(solution)/shard_map/reshape | solution.py:102
  407.0 9.0 %reduce.14 = bf16[1024,512]{1,0:T(8,128)(2,1)} reduce(bf16[1024,1,512]{2,1,0:T(2,128)(2,1)} %bitcast.145, bf16[]{:T(256)} %broadcast.182), dimensions={1}, to_apply=%bitcast.115.reduce_sub_computation | reduce | bytes 2097154
  416.0 2.6 reshape.236
  418.6 6.2 %all-to-all-start.6 = ((bf16[8,2,32768]{2,1,0:T(2,128)(2,1)}), bf16[8,2,32768]{2,1,0:T(2,128)(2,1)}, u32[]{:S(2)}, u32[]{:S(2)}) async-start(bf16[8,2,32768]{2,1,0:T(2,128)(2,1)} %reshape.236), calls=%async_computation.6 | async-start | bytes 2097152 | tf_op jit(solution)/shard_map/all_to_all | solution.py:142
  426.7 3.7 convolution_convert_fusion
  431.1 3.9 copy.149
  435.0 9.2 %reduce.13 = bf16[1024,512]{1,0:T(8,128)(2,1)} reduce(bf16[1024,1,512]{2,1,0:T(2,128)(2,1)} %bitcast.146, bf16[]{:T(256)} %broadcast.182), dimensions={1}, to_apply=%bitcast.113.reduce_sub_computation | reduce | bytes 2097154
  444.2 2.6 reshape.234
  446.8 3.6 all-to-all-done.6
  450.3 4.5 all-to-all-start.5
  456.7 4.1 add_convert_fusion
  460.8 4.6 copy.159
  465.4 8.0 %reduce.15 = bf16[1024,512]{1,0:T(8,128)(2,1)} reduce(bf16[1024,1,512]{2,1,0:T(2,128)(2,1)S(1)} %bitcast.142, bf16[]{:T(256)} %broadcast.182), dimensions={1}, to_apply=%bitcast.117.reduce_sub_computation | reduce | bytes 2097154
  473.4 2.6 reshape.238
  476.0 4.2 all-to-all-done.5
  480.2 4.5 all-to-all-start.7
  484.7 4.3 reshape.231
  490.3 2.3 copy.142
  492.5 4.3 reshape.237
  501.0 4.3 reshape.235
  510.1 4.3 reshape.239
  518.6 8.5 %fusion.3 = bf16[128,2048]{1,0:T(8,128)(2,1)S(1)} fusion(bf16[128,4096]{0,1:T(8,128)(2,1)} %bitcast.177, bf16[2,4096,2048]{2,1,0:T(8,128)(2,1)} %all-gather.2.cloned.1.call-done), kind=kOutput, calls=%fused_computation.5 | convolution fusion | flops 2147483648 | bytes 18350080 | tf_op jit(solution)/shard_map/dot_general | solution.py:126
  527.2 9.0 %fusion.17 = bf16[1,128,2048]{2,1,0:T(8,128)(2,1)} fusion(bf16[128,2048]{1,0:T(8,128)(2,1)S(1)} %fusion.3, bf16[128,4096]{0,1:T(8,128)(2,1)S(1)} %bitcast.178, bf16[2,4096,2048]{2,1,0:T(8,128)(2,1)} %all-gather.2.cloned.1.call-done, pred[128]{0:T(512)(128)(4,1)S(1)} %compare_bitcast_fusion), kind=kOutput, calls=%fused_computation.26 | convolution fusion | flops 2147745792 | bytes 18874496 | tf_op jit(solution)/shard_map/dot_general | solution.py:125
  (74 shorter events, 42.5 us)
Async XLA Ops:
  7.2 254.7 %copy-start = (bf16[1,128,2048]{2,1,0:T(8,128)(2,1)S(1)}, bf16[1,128,2048]{2,1,0:T(8,128)(2,1)}, u32[]{:S(2)}) copy-start(bf16[1,128,2048]{2,1,0:T(8,128)(2,1)} %param.23) | copy-start | bytes 1572868
  7.2 254.7 %all-gather.2.cloned.1.call-start = ((), (), s32[]{:S(2)}) async-start(), calls=%async_computation.8 | async-start | bytes 34603008 | tf_op jit(solution)/shard_map/all_gather | solution.py:124
  39.0 54.2 %all-to-all-start = ((bf16[8,2,32768]{2,1,0:T(2,128)(2,1)}), bf16[8,2,32768]{2,1,0:T(2,128)(2,1)}, u32[]{:S(2)}, u32[]{:S(2)}) async-start(bf16[8,2,32768]{2,1,0:T(2,128)(2,1)} %reshape.224), calls=%async_computation | async-start | bytes 2097152 | tf_op jit(solution)/shard_map/all_to_all | solution.py:113
  93.2 46.7 %all-to-all-start.1 = ((bf16[8,2,32768]{2,1,0:T(2,128)(2,1)}), bf16[8,2,32768]{2,1,0:T(2,128)(2,1)}, u32[]{:S(2)}, u32[]{:S(2)}) async-start(bf16[8,2,32768]{2,1,0:T(2,128)(2,1)} %reshape.226), calls=%async_computation.1 | async-start | bytes 2097152 | tf_op jit(solution)/shard_map/all_to_all | solution.py:114
  100.6 30.7 %copy-start.15 = (s32[1,128]{1,0:T(1,128)S(1)}, s32[1,128]{1,0:T(1,128)}, u32[]{:S(2)}) copy-start(s32[1,128]{1,0:T(1,128)} %param.21) | copy-start | bytes 1540
  139.9 176.4 %all-to-all-start.2 = ((bf16[8,2,32768]{2,1,0:T(2,128)(2,1)}), bf16[8,2,32768]{2,1,0:T(2,128)(2,1)}, u32[]{:S(2)}, u32[]{:S(2)}) async-start(bf16[8,2,32768]{2,1,0:T(2,128)(2,1)} %reshape.228), calls=%async_computation.2 | async-start | bytes 2097152 | tf_op jit(solution)/shard_map/all_to_all | solution.py:115
  149.7 3.6 copy-start.5
  153.3 5.3 copy-start.10
  316.3 30.7 %all-to-all-start.4 = ((bf16[8,2,32768]{2,1,0:T(2,128)(2,1)}), bf16[8,2,32768]{2,1,0:T(2,128)(2,1)}, u32[]{:S(2)}, u32[]{:S(2)}) async-start(bf16[8,2,32768]{2,1,0:T(2,128)(2,1)} %reshape.232), calls=%async_computation.4 | async-start | bytes 2097152 | tf_op jit(solution)/shard_map/all_to_all | solution.py:133
  330.4 6.2 %copy-start.6 = (bf16[1024,4,128]{2,0,1:T(8,128)(2,1)S(1)}, bf16[1024,4,128]{2,0,1:T(8,128)(2,1)}, u32[]{:S(2)}) copy-start(bf16[1024,4,128]{2,0,1:T(8,128)(2,1)} %copy.132) | copy-start | bytes 3145732
  330.4 6.2 %copy-start.11 = (bf16[1024,4,128]{2,0,1:T(8,128)(2,1)S(1)}, bf16[1024,4,128]{2,0,1:T(8,128)(2,1)}, u32[]{:S(2)}) copy-start(bf16[1024,4,128]{2,0,1:T(8,128)(2,1)} %copy-done.10) | copy-start | bytes 3145732
  336.6 2.2 copy-start.2
  336.6 2.5 copy-start.13
  342.5 1.9 copy-start.8
  345.1 15.7 %copy-start.3 = (bf16[4,512,512]{1,2,0:T(8,128)(2,1)}, bf16[4,512,512]{1,2,0:T(8,128)(2,1)S(1)}, u32[]{:S(2)}) copy-start(bf16[4,512,512]{1,2,0:T(8,128)(2,1)S(1)} %fusion.21) | copy-start | bytes 6291460
  360.7 2.8 copy-start.9
  386.7 31.9 %all-to-all-start.3 = ((bf16[8,2,32768]{2,1,0:T(2,128)(2,1)}), bf16[8,2,32768]{2,1,0:T(2,128)(2,1)}, u32[]{:S(2)}, u32[]{:S(2)}) async-start(bf16[8,2,32768]{2,1,0:T(2,128)(2,1)} %reshape.230), calls=%async_computation.3 | async-start | bytes 2097152 | tf_op jit(solution)/shard_map/all_to_all | solution.py:122
  393.2 5.5 %copy-start.7 = (bf16[1024,4,128]{2,0,1:T(8,128)(2,1)S(1)}, bf16[1024,4,128]{2,0,1:T(8,128)(2,1)}, u32[]{:S(2)}) copy-start(bf16[1024,4,128]{2,0,1:T(8,128)(2,1)} %copy.132) | copy-start | bytes 3145732
  398.7 2.3 copy-start.12
  418.6 31.8 %all-to-all-start.6 = ((bf16[8,2,32768]{2,1,0:T(2,128)(2,1)}), bf16[8,2,32768]{2,1,0:T(2,128)(2,1)}, u32[]{:S(2)}, u32[]{:S(2)}) async-start(bf16[8,2,32768]{2,1,0:T(2,128)(2,1)} %reshape.236), calls=%async_computation.6 | async-start | bytes 2097152 | tf_op jit(solution)/shard_map/all_to_all | solution.py:142
  435.0 19.8 %copy-start.4 = (bf16[4,512,512]{1,2,0:T(8,128)(2,1)S(1)}, bf16[4,512,512]{1,2,0:T(8,128)(2,1)}, u32[]{:S(2)}) copy-start(bf16[4,512,512]{1,2,0:T(8,128)(2,1)} %copy-done.3) | copy-start | bytes 6291460
  450.3 29.9 %all-to-all-start.5 = ((bf16[8,2,32768]{2,1,0:T(2,128)(2,1)}), bf16[8,2,32768]{2,1,0:T(2,128)(2,1)}, u32[]{:S(2)}, u32[]{:S(2)}) async-start(bf16[8,2,32768]{2,1,0:T(2,128)(2,1)} %reshape.234), calls=%async_computation.5 | async-start | bytes 2097152 | tf_op jit(solution)/shard_map/all_to_all | solution.py:139
  480.2 29.9 %all-to-all-start.7 = ((bf16[8,2,32768]{2,1,0:T(2,128)(2,1)}), bf16[8,2,32768]{2,1,0:T(2,128)(2,1)}, u32[]{:S(2)}, u32[]{:S(2)}) async-start(bf16[8,2,32768]{2,1,0:T(2,128)(2,1)} %reshape.238), calls=%async_computation.7 | async-start | bytes 2097152 | tf_op jit(solution)/shard_map/all_to_all | solution.py:145
  518.6 8.5 %copy-start.14 = (bf16[1,128,8,512]{1,3,2,0:T(8,128)(2,1)S(1)}, bf16[1,128,8,512]{1,3,2,0:T(8,128)(2,1)}, u32[]{:S(2)}) copy-start(bf16[1,128,8,512]{1,3,2,0:T(8,128)(2,1)} %copy.142) | copy-start | bytes 3145732
  527.2 9.1 %copy-start.1 = (bf16[1,128,2048]{2,1,0:T(8,128)(2,1)S(1)}, bf16[1,128,2048]{2,1,0:T(8,128)(2,1)}, u32[]{:S(2)}) copy-start(bf16[1,128,2048]{2,1,0:T(8,128)(2,1)} %param.23) | copy-start | bytes 1572868
Sparse Core Ops, SparseCore 0:
  11.0 250.7 all-gather.1
where the time goes:
time: 554 us; the launch traced here: 544 us
  local copies, waits for them, and re-layouts  140 us (25%)
  other arithmetic  139 us (25%)
  waiting for transfers between devices  132 us (24%)
  matrix products  74.5 us (13%)
  starting transfers between devices  44 us (8%)
  between operations  15 us (3%)
    unnamed x8, other arithmetic  129 us
    all_gather x1, waiting for transfers between devices, per_device(): lax.all_gather(out_weight, ('fsdp', 'ctx'), axis=1, tiled=True)  103 us
    unnamed x63, local copies, waits for them, and re-layouts  85.6 us
    dot_general x2, matrix products, transposed_product(): lax.dot_general(left, right, (((1,), (1,)), ((), ())), preferred_element_...  23.7 us
    reshape x4, local copies, waits for them, and re-layouts, heads_last(): return stacked.transpose(1, 0, 2).reshape(1, length, local_width)  20.6 us
    all_to_all x1, waiting for transfers between devices, per_device(): lax.all_to_all(query_proj, 'ctx', split_axis=2, concat_axis=1, tiled=True)  16.4 us
    reshape x8, local copies, waits for them, and re-layouts, heads_first(): return flat.reshape(length, local_heads, HEAD_SIZE).transpose(1, 0, 2)  13.8 us
  transfers between devices with their start and end apart: 9, of which 7 were waited for; matrix products, arithmetic and copies ran while one was open for 52% of the time, Pallas kernels for 0%

commit v1 on v0

--- a/solution.py
+++ b/solution.py
@@ -1,6 +1,8 @@
 import jax
 import jax.numpy as jnp
 from jax import lax
+from jax.experimental import pallas as pl
+from jax.experimental.pallas import tpu as pltpu
 from jax.sharding import PartitionSpec as P
 
 HEAD_SIZE = 128
@@ -102,7 +104,7 @@
     return stacked.transpose(1, 0, 2).reshape(1, length, local_width)
 
 
-def per_device(query_proj, key_proj, value_proj, modality, out_weight, grad_projected):
+def per_device_gathered(query_proj, key_proj, value_proj, modality, out_weight, grad_projected):
     context_size = lax.axis_size("ctx")
     row_count = query_proj.shape[1]
     inner_width = query_proj.shape[2]
@@ -149,6 +151,109 @@
     return (projected, grad_query, grad_key, grad_value)
 
 
+def fused_attention_kernel(
+    q_ref, k_ref, v_ref, g_ref, a_ref, dq_ref, dk_ref, dv_ref, dk_sum, dv_sum
+):
+    length = q_ref.shape[0]
+    rows = min(256, length)
+    scaling = HEAD_SIZE ** (-0.5)
+    nt = (((1,), (1,)), ((), ()))
+    tn = (((0,), (0,)), ((), ()))
+    for block in reversed(range(length // rows)):
+        offset = block * rows
+        finish = offset + rows
+        q = q_ref[offset:finish, :]
+        g = g_ref[offset:finish, :]
+        k = k_ref[:finish, :]
+        v = v_ref[:finish, :]
+        scores = lax.dot_general(q, k, nt, preferred_element_type=jnp.float32) * scaling
+        places = lax.broadcasted_iota(jnp.int32, scores.shape, 0) + offset
+        scores = jnp.where(
+            lax.broadcasted_iota(jnp.int32, scores.shape, 1) <= places, scores, -jnp.inf
+        )
+        raised = jnp.exp(scores - jnp.max(scores, axis=-1, keepdims=True))
+        weights = raised * (1.0 / jnp.sum(raised, axis=-1, keepdims=True))
+        weights_bf = weights.astype(jnp.bfloat16)
+        attention = jnp.dot(weights_bf, v, preferred_element_type=jnp.float32).astype(jnp.bfloat16)
+        a_ref[offset:finish, :] = attention
+        delta = jnp.sum(
+            g.astype(jnp.float32) * attention.astype(jnp.float32), axis=-1, keepdims=True
+        )
+        grad_weights = lax.dot_general(g, v, nt, preferred_element_type=jnp.float32)
+        grad_scores = (weights * (grad_weights - delta) * scaling).astype(jnp.bfloat16)
+        dq_ref[offset:finish, :] = jnp.dot(
+            grad_scores, k, preferred_element_type=jnp.float32
+        ).astype(jnp.bfloat16)
+        dk = lax.dot_general(grad_scores, q, tn, preferred_element_type=jnp.float32)
+        dv = lax.dot_general(weights_bf, g, tn, preferred_element_type=jnp.float32)
+        if finish == length:
+            dk_sum[...] = dk
+            dv_sum[...] = dv
+        else:
+            dk_sum[:finish, :] += dk
+            dv_sum[:finish, :] += dv
+    dk_ref[...] = dk_sum[...].astype(jnp.bfloat16)
+    dv_ref[...] = dv_sum[...].astype(jnp.bfloat16)
+
+
+def fused_attention(q, k, v, g):
+    length, width = q.shape
+    spec = pl.BlockSpec((length, HEAD_SIZE), lambda h: (0, h))
+    return pl.pallas_call(
+        fused_attention_kernel,
+        grid=(width // HEAD_SIZE,),
+        in_specs=[spec] * 4,
+        out_specs=[spec] * 4,
+        out_shape=[jax.ShapeDtypeStruct(q.shape, jnp.bfloat16)] * 4,
+        scratch_shapes=[pltpu.VMEM((length, HEAD_SIZE), jnp.float32)] * 2,
+        compiler_params=pltpu.CompilerParams(vmem_limit_bytes=48 * 2**20),
+        cost_estimate=pl.CostEstimate(
+            flops=9 * length * length * width, bytes_accessed=16 * length * width, transcendentals=0
+        ),
+    )(q, k, v, g)
+
+
+def per_device(query_proj, key_proj, value_proj, modality, out_weight, grad_projected):
+    context_size = lax.axis_size("ctx")
+    groups = lax.axis_size("fsdp")
+    row_count = query_proj.shape[1]
+    piece = out_weight.shape[1]
+    length = row_count * context_size
+    width = groups * piece
+
+    def to_heads(flat):
+        split = flat[0].reshape(row_count, groups, context_size, piece).transpose(2, 0, 1, 3)
+        return lax.all_to_all(split, "ctx", 0, 0).reshape(length, width)
+
+    def to_rows(flat):
+        split = lax.all_to_all(
+            flat.reshape(context_size, row_count, groups, piece), "ctx", 0, 0
+        )
+        return split.transpose(1, 2, 0, 3).reshape(1, row_count, width * context_size)
+
+    weight = lax.all_gather(out_weight, "fsdp", axis=1, tiled=True).reshape(2 * width, -1)
+    upstream = lax.all_gather(grad_projected[0], "ctx", axis=0, tiled=True)
+    image = (lax.all_gather(modality[0], "ctx", axis=0, tiled=True) == 1)[:, None]
+    both = transposed_product(upstream, weight)
+    grad_attention = jnp.where(image, both[:, width:], both[:, :width]).astype(jnp.bfloat16)
+    attention, grad_q, grad_k, grad_v = fused_attention(
+        to_heads(query_proj), to_heads(key_proj), to_heads(value_proj), grad_attention
+    )
+    zero = jnp.zeros_like(attention)
+    spread = jnp.concatenate(
+        [jnp.where(image, zero, attention), jnp.where(image, attention, zero)], axis=1
+    )
+    partial = jnp.dot(spread, weight, preferred_element_type=jnp.float32).astype(jnp.bfloat16)
+    partial = lax.all_to_all(partial.reshape(context_size, row_count, -1), "ctx", 0, 0)
+    projected = jnp.sum(partial.astype(jnp.float32), axis=0).astype(jnp.bfloat16)[None]
+    return projected, to_rows(grad_q), to_rows(grad_k), to_rows(grad_v)
+
+
+def aligned(mesh, query_shape, weight_shape):
+    devices = mesh.shape["fsdp"] * mesh.shape["ctx"]
+    return (weight_shape[1] // devices) % HEAD_SIZE == 0 and query_shape[1] <= 2048
+
+
 def solution(mesh):
     placed = (
         P("fsdp", "ctx", None),
@@ -158,15 +263,14 @@
         P(None, ("fsdp", "ctx"), None),
         P("fsdp", "ctx", None),
     )
-    return jax.shard_map(
-        per_device,
-        mesh=mesh,
-        in_specs=placed,
-        out_specs=(
-            P("fsdp", "ctx", None),
-            P("fsdp", "ctx", None),
-            P("fsdp", "ctx", None),
-            P("fsdp", "ctx", None),
-        ),
-        check_vma=False,
-    )
+    def whole(*arrays):
+        local = per_device if aligned(mesh, arrays[0].shape, arrays[4].shape) else per_device_gathered
+        return jax.shard_map(
+            local,
+            mesh=mesh,
+            in_specs=placed,
+            out_specs=(P("fsdp", "ctx", None),) * 4,
+            check_vma=False,
+        )(*arrays)
+
+    return whole

time: 554 us -> 386 us (0.70); the launches traced: 544 us -> 385 us
  other arithmetic: 139 us -> 5.26 us
  local copies, waits for them, and re-layouts: 140 us -> 26.1 us
  waiting for transfers between devices: 132 us -> 218 us
  matrix products: 74.5 us -> 16.3 us
  blocking collectives: 0 us -> 49.3 us
  Pallas kernels: 0 us -> 18.3 us
  starting transfers between devices: 44 us -> 37.4 us
    all_to_all x8 -> x7, waiting for transfers between devices: 27.9 us -> 213 us  [the longest x1 83.7 us: per_device(): lax.all_to_all(partial.reshape(context_size, row_count, -1), 'ctx', 0, 0)]
    unnamed x8 -> x0, other arithmetic: 129 us -> none
    all_gather x1 -> x2, waiting for transfers between devices: 103 us -> 4.31 us  [the longest x1 4.31 us: per_device(): upstream = lax.all_gather(grad_projected[0], 'ctx', axis=0, tiled=True)]
    unnamed x63 -> x16, local copies, waits for them, and re-layouts: 85.6 us -> 8.8 us
    all_gather x0 -> x1, blocking collectives: none -> 49.3 us  [per_device(): lax.all_gather(modality[0], 'ctx', axis=0, tiled=True) == 1]
    dot_general x13 -> x1, matrix products: 45.5 us -> 8.26 us  [per_device(): jnp.dot(spread, weight, preferred_element_type=jnp.float32)]
    reshape x12 -> x6, local copies, waits for them, and re-layouts: 34.4 us -> 8.26 us  [the longest x3 4.44 us: to_rows(): flat.reshape(context_size, row_count, groups, piece)]
    pallas_call x0 -> x1, Pallas kernels: none -> 18.3 us  [fused_attention(): pl.pallas_call(fused_attention_kernel, grid=(width // HEAD_SIZE,), in_spe...]
  transfers between devices with their start and end apart: 9 -> 9, of which waited for: 7 -> 8; matrix products, arithmetic and copies ran while one was open for 52% -> 8% of each run, Pallas kernels for 0% -> 0%
where the time goes in v1:
time: 386 us; the launch traced here: 385 us
  waiting for transfers between devices  218 us (56%)
  blocking collectives  49.3 us (13%)
  starting transfers between devices  37.4 us (10%)
  local copies, waits for them, and re-layouts  26.1 us (7%)
  Pallas kernels  18.3 us (5%)
  matrix products  16.3 us (4%)
  between operations  14.2 us (4%)
  other arithmetic  5.26 us (1%)
    all_to_all x1, waiting for transfers between devices, per_device(): lax.all_to_all(partial.reshape(context_size, row_count, -1), 'ctx', 0, 0)  83.7 us
    all_to_all x3, waiting for transfers between devices, to_heads(): return lax.all_to_all(split, 'ctx', 0, 0).reshape(length, width)  65.1 us
    all_to_all x3, waiting for transfers between devices, to_rows(): lax.all_to_all(flat.reshape(context_size, row_count, groups, piece), 'ctx...  63.7 us
    all_gather x1, blocking collectives, per_device(): lax.all_gather(modality[0], 'ctx', axis=0, tiled=True) == 1  49.3 us
    pallas_call x1, Pallas kernels, fused_attention(): pl.pallas_call(fused_attention_kernel, grid=(width // HEAD_SIZE,), in_spe...  18.3 us
    all_to_all x3, starting transfers between devices, to_heads(): return lax.all_to_all(split, 'ctx', 0, 0).reshape(length, width)  16.6 us
    all_to_all x3, starting transfers between devices, to_rows(): lax.all_to_all(flat.reshape(context_size, row_count, groups, piece), 'ctx...  16.2 us
    unnamed x16, local copies, waits for them, and re-layouts  8.8 us
  transfers between devices with their start and end apart: 9, of which 8 were waited for; matrix products, arithmetic and copies ran while one was open for 8% of the time, Pallas kernels for 0%

profile of v1, /device:TPU:0, one launch (start us, length us, event | category | flops | bytes accessed | tf_op | source)
XLA Modules:
  0.0 385.0 jit_solution(17549666239320635694)
XLA Ops:
  7.2 0.0 copy-start.3
  7.2 0.0 all-gather.5.cloned.1.call-start
  7.2 0.7 all-gather.5.cloned.1.call-update
  7.9 0.0 all-gather.7.cloned.1.call-start
  8.0 0.7 all-gather.7.cloned.1.call-update
  8.7 1.5 copy.16
  10.1 1.4 copy.33
  11.5 7.3 %all-to-all-start = ((bf16[8,128,4,128]{3,2,1,0:T(4,128)(2,1)}), bf16[8,128,4,128]{3,2,1,0:T(4,128)(2,1)S(1)}, u32[]{:S(2)}, u32[]{:S(2)}) async-start(bf16[8,128,4,128]{3,2,1,0:T(4,128)(2,1)} %bitcast.52), calls=%async_computation | async-start | bytes 2097152 | tf_op jit(solution)/shard_map/all_to_all | solution.py:226
  18.8 0.0 copy-done.3
  18.8 0.2 copy.18
  19.0 1.4 copy.32
  20.4 24.1 %all-to-all-done = bf16[8,128,4,128]{3,2,1,0:T(4,128)(2,1)S(1)} async-done(((bf16[8,128,4,128]{3,2,1,0:T(4,128)(2,1)}), bf16[8,128,4,128]{3,2,1,0:T(4,128)(2,1)S(1)}, u32[]{:S(2)}, u32[]{:S(2)}) %all-to-all-start) | async-done | bytes 1048608 | tf_op jit(solution)/shard_map/all_to_all | solution.py:226
  44.5 0.0 copy-start.4
  44.5 3.7 all-to-all-start.1
  48.3 1.4 copy.20
  49.7 1.4 copy.31
  51.1 38.1 %all-to-all-done.1 = bf16[8,128,4,128]{3,2,1,0:T(4,128)(2,1)S(1)} async-done(((bf16[8,128,4,128]{3,2,1,0:T(4,128)(2,1)}), bf16[8,128,4,128]{3,2,1,0:T(4,128)(2,1)S(1)}, u32[]{:S(2)}, u32[]{:S(2)}) %all-to-all-start.1) | async-done | bytes 1048608 | tf_op jit(solution)/shard_map/all_to_all | solution.py:226
  89.2 5.6 %all-to-all-start.2 = ((bf16[8,128,4,128]{3,2,1,0:T(4,128)(2,1)}), bf16[8,128,4,128]{3,2,1,0:T(4,128)(2,1)}, u32[]{:S(2)}, u32[]{:S(2)}) async-start(bf16[8,128,4,128]{3,2,1,0:T(4,128)(2,1)} %bitcast.50), calls=%async_computation.2 | async-start | bytes 2097152 | tf_op jit(solution)/shard_map/all_to_all | solution.py:226
  94.7 0.0 copy-done.4
  94.7 49.3 %all-gather = s32[1,1024]{1,0:T(1,128)S(1)} all-gather(s32[1,128]{1,0:T(1,128)S(1)} %copy-done.4), channel_id=2, replica_groups=mesh['fsdp'=4,'ctx'=8] {'ctx'}, dimensions={1}, use_global_device_ids=true | all-gather | bytes 4608 | tf_op jit(solution)/shard_map/all_gather | solution.py:236
  144.1 0.2 copy.30
  144.3 1.2 copy.29
  145.4 2.9 all-to-all-done.2
  148.3 2.4 copy.28
  150.7 0.0 all-gather.5.cloned.1.call-done
  150.7 4.3 %all-gather.7.cloned.1.call-done = bf16[1,1024,2048]{2,1,0:T(8,128)(2,1)} async-done(((bf16[1,128,2048]{2,1,0:T(8,128)(2,1)}), bf16[1,1024,2048]{2,1,0:T(8,128)(2,1)}) %all-gather.7.cloned.1.call-update) | async-done | bytes 4194320 | tf_op jit(solution)/shard_map/all_gather | solution.py:235
  155.0 8.0 %fusion = bf16[1024,1024]{1,0:T(8,128)(2,1)S(1)} fusion(bf16[1024,2048]{1,0:T(8,128)(2,1)} %bitcast.68, bf16[1,1024,2048]{2,1,0:T(8,128)(2,1)} %all-gather.7.cloned.1.call-done), kind=kOutput, calls=%fused_computation | convolution fusion | flops 4294967296 | bytes 10485760 | tf_op jit(solution)/shard_map/dot_general | solution.py:94
  163.0 1.2 fusion.2.g_ref
  164.2 18.3 %shard_map.93 = (bf16[1024,512]{1,0:T(8,128)(2,1)S(1)}, bf16[1024,512]{1,0:T(8,128)(2,1)S(1)}, bf16[1024,512]{1,0:T(8,128)(2,1)S(1)}, bf16[1024,512]{1,0:T(8,128)(2,1)S(1)}) custom-call(bf16[1024,512]{1,0:T(8,128)(2,1)S(1)} %bitcast.53, bf16[1024,512]{1,0:T(8,128)(2,1)} %bitcast.65, bf16[1024,512]{1,0:T(8,128)(2,1)} %bitcast.66, bf16[1024,512]{1,0:T(8,128)(2,1)} %fusion.2.g_ref), custom_call_target="tpu_custom_call" | custom-call | flops 4831838208 | bytes 8388608 | tf_op jit(solution)/shard_map/pallas_call | solution.py:202
  182.5 0.0 copy-start
  182.5 1.0 copy-done
  183.5 0.0 copy-start.2
  183.5 1.0 copy-done.2
  184.4 0.0 copy-start.1
  184.4 2.2 reshape.47
  186.7 8.9 %all-to-all-start.4 = ((bf16[8,128,4,128]{3,2,1,0:T(4,128)(2,1)}), bf16[8,128,4,128]{3,2,1,0:T(4,128)(2,1)}, u32[]{:S(2)}, u32[]{:S(2)}) async-start(bf16[8,128,4,128]{3,2,1,0:T(4,128)(2,1)} %reshape.47), calls=%async_computation.4 | async-start | bytes 2097152 | tf_op jit(solution)/shard_map/all_to_all | solution.py:229
  195.6 0.0 copy-done.1
  195.6 1.1 reshape.49
  196.7 22.5 %all-to-all-done.4 = bf16[8,128,4,128]{3,2,1,0:T(4,128)(2,1)} async-done(((bf16[8,128,4,128]{3,2,1,0:T(4,128)(2,1)}), bf16[8,128,4,128]{3,2,1,0:T(4,128)(2,1)}, u32[]{:S(2)}, u32[]{:S(2)}) %all-to-all-start.4) | async-done | bytes 1048608 | tf_op jit(solution)/shard_map/all_to_all | solution.py:229
  219.2 3.6 all-to-all-start.5
  222.8 1.1 reshape.51
  223.9 24.0 %all-to-all-done.5 = bf16[8,128,4,128]{3,2,1,0:T(4,128)(2,1)S(1)} async-done(((bf16[8,128,4,128]{3,2,1,0:T(4,128)(2,1)}), bf16[8,128,4,128]{3,2,1,0:T(4,128)(2,1)S(1)}, u32[]{:S(2)}, u32[]{:S(2)}) %all-to-all-start.5) | async-done | bytes 1048608 | tf_op jit(solution)/shard_map/all_to_all | solution.py:229
  247.9 3.7 all-to-all-start.6
  251.7 0.2 broadcast_select_fusion.1
  251.9 8.3 %convolution_convert_fusion = bf16[1024,2048]{1,0:T(8,128)(2,1)} fusion(bf16[1024,2048]{1,0:T(8,128)(2,1)} %bitcast.69, bf16[1024,512]{1,0:T(8,128)(2,1)S(1)} %get-tuple-element.13, bf16[1024,512]{1,0:T(8,128)(2,1)S(1)} %get-tuple-element.12), kind=kOutput, calls=%fused_computation.2 | convolution fusion | flops 4301258752 | bytes 10485760 | tf_op jit(solution)/shard_map/dot_general | solution.py:246
  260.1 17.2 %all-to-all-done.6 = bf16[8,128,4,128]{3,2,1,0:T(4,128)(2,1)S(1)} async-done(((bf16[8,128,4,128]{3,2,1,0:T(4,128)(2,1)}), bf16[8,128,4,128]{3,2,1,0:T(4,128)(2,1)S(1)}, u32[]{:S(2)}, u32[]{:S(2)}) %all-to-all-start.6) | async-done | bytes 1048608 | tf_op jit(solution)/shard_map/all_to_all | solution.py:229
  277.3 4.6 %all-to-all-start.3 = ((bf16[8,128,2048]{2,1,0:T(8,128)(2,1)}), bf16[8,128,2048]{2,1,0:T(8,128)(2,1)}, u32[]{:S(2)}, u32[]{:S(2)}) async-start(bf16[8,128,2048]{2,1,0:T(8,128)(2,1)} %bitcast.54), calls=%async_computation.3 | async-start | bytes 8388608 | tf_op jit(solution)/shard_map/all_to_all | solution.py:247
  281.9 2.4 copy.13
  284.3 1.3 reshape.48
  285.6 1.2 copy.14
  286.8 1.3 reshape.50
  288.1 1.2 copy.15
  289.3 1.3 reshape.52
  290.6 83.7 %all-to-all-done.3 = bf16[8,128,2048]{2,1,0:T(8,128)(2,1)} async-done(((bf16[8,128,2048]{2,1,0:T(8,128)(2,1)}), bf16[8,128,2048]{2,1,0:T(8,128)(2,1)}, u32[]{:S(2)}, u32[]{:S(2)}) %all-to-all-start.3) | async-done | bytes 4194336 | tf_op jit(solution)/shard_map/all_to_all | solution.py:247
  374.3 3.8 reduce_sum.12
  (1 shorter events, 0.0 us)
Async XLA Ops:
  7.2 11.6 %copy-start.3 = (bf16[1,128,4096]{2,1,0:T(8,128)(2,1)S(1)}, bf16[1,128,4096]{2,1,0:T(8,128)(2,1)}, u32[]{:S(2)}) copy-start(bf16[1,128,4096]{2,1,0:T(8,128)(2,1)} %param.7) | copy-start | bytes 3145732
  7.2 143.6 %all-gather.5.cloned.1.call-start = ((), (), s32[]{:S(2)}) async-start(), calls=%async_computation.7 | async-start | bytes 5242880 | tf_op jit(solution)/shard_map/all_gather | solution.py:234
  7.9 147.1 %all-gather.7.cloned.1.call-start = ((), (), s32[]{:S(2)}) async-start(), calls=%async_computation.8 | async-start | bytes 4718592 | tf_op jit(solution)/shard_map/all_gather | solution.py:235
  11.5 33.0 %all-to-all-start = ((bf16[8,128,4,128]{3,2,1,0:T(4,128)(2,1)}), bf16[8,128,4,128]{3,2,1,0:T(4,128)(2,1)S(1)}, u32[]{:S(2)}, u32[]{:S(2)}) async-start(bf16[8,128,4,128]{3,2,1,0:T(4,128)(2,1)} %bitcast.52), calls=%async_computation | async-start | bytes 2097152 | tf_op jit(solution)/shard_map/all_to_all | solution.py:226
  44.5 50.2 %copy-start.4 = (s32[1,128]{1,0:T(1,128)S(1)}, s32[1,128]{1,0:T(1,128)}, u32[]{:S(2)}) copy-start(s32[1,128]{1,0:T(1,128)} %param.9) | copy-start | bytes 1540
  44.5 44.6 %all-to-all-start.1 = ((bf16[8,128,4,128]{3,2,1,0:T(4,128)(2,1)}), bf16[8,128,4,128]{3,2,1,0:T(4,128)(2,1)S(1)}, u32[]{:S(2)}, u32[]{:S(2)}) async-start(bf16[8,128,4,128]{3,2,1,0:T(4,128)(2,1)} %bitcast.51), calls=%async_computation.1 | async-start | bytes 2097152 | tf_op jit(solution)/shard_map/all_to_all | solution.py:226
  89.2 59.2 %all-to-all-start.2 = ((bf16[8,128,4,128]{3,2,1,0:T(4,128)(2,1)}), bf16[8,128,4,128]{3,2,1,0:T(4,128)(2,1)}, u32[]{:S(2)}, u32[]{:S(2)}) async-start(bf16[8,128,4,128]{3,2,1,0:T(4,128)(2,1)} %bitcast.50), calls=%async_computation.2 | async-start | bytes 2097152 | tf_op jit(solution)/shard_map/all_to_all | solution.py:226
  182.5 1.0 copy-start
  183.5 1.0 copy-start.2
  184.4 11.2 %copy-start.1 = (bf16[1024,512]{1,0:T(8,128)(2,1)S(1)}, bf16[1024,512]{1,0:T(8,128)(2,1)}, u32[]{:S(2)}) copy-start(bf16[1024,512]{1,0:T(8,128)(2,1)} %copy-done) | copy-start | bytes 3145732
  186.7 32.6 %all-to-all-start.4 = ((bf16[8,128,4,128]{3,2,1,0:T(4,128)(2,1)}), bf16[8,128,4,128]{3,2,1,0:T(4,128)(2,1)}, u32[]{:S(2)}, u32[]{:S(2)}) async-start(bf16[8,128,4,128]{3,2,1,0:T(4,128)(2,1)} %reshape.47), calls=%async_computation.4 | async-start | bytes 2097152 | tf_op jit(solution)/shard_map/all_to_all | solution.py:229
  219.2 28.7 %all-to-all-start.5 = ((bf16[8,128,4,128]{3,2,1,0:T(4,128)(2,1)}), bf16[8,128,4,128]{3,2,1,0:T(4,128)(2,1)S(1)}, u32[]{:S(2)}, u32[]{:S(2)}) async-start(bf16[8,128,4,128]{3,2,1,0:T(4,128)(2,1)} %reshape.49), calls=%async_computation.5 | async-start | bytes 2097152 | tf_op jit(solution)/shard_map/all_to_all | solution.py:229
  247.9 29.4 %all-to-all-start.6 = ((bf16[8,128,4,128]{3,2,1,0:T(4,128)(2,1)}), bf16[8,128,4,128]{3,2,1,0:T(4,128)(2,1)S(1)}, u32[]{:S(2)}, u32[]{:S(2)}) async-start(bf16[8,128,4,128]{3,2,1,0:T(4,128)(2,1)} %reshape.51), calls=%async_computation.6 | async-start | bytes 2097152 | tf_op jit(solution)/shard_map/all_to_all | solution.py:229
  277.3 97.0 %all-to-all-start.3 = ((bf16[8,128,2048]{2,1,0:T(8,128)(2,1)}), bf16[8,128,2048]{2,1,0:T(8,128)(2,1)}, u32[]{:S(2)}, u32[]{:S(2)}) async-start(bf16[8,128,2048]{2,1,0:T(8,128)(2,1)} %bitcast.54), calls=%async_computation.3 | async-start | bytes 8388608 | tf_op jit(solution)/shard_map/all_to_all | solution.py:247
Sparse Core Ops, SparseCore 0:
  9.5 37.1 all-gather.4
  48.9 106.1 all-gather.6

commit v2 on v1

--- a/solution.py
+++ b/solution.py
@@ -213,6 +213,165 @@
     )(q, k, v, g)
 
 
+def exchange(arrays, kinds, collective_id):
+    size, groups = lax.axis_size("ctx"), lax.axis_size("fsdp")
+    places = size // 2
+    spans = {
+        "deal": size, "ctx": size, "chain": size, "fsdp": groups, "line": places, "swap": 2
+    }
+    count = len(arrays)
+
+    def block_shape(a, kind):
+        if kind in ("deal", "line"):
+            return a.shape[1:]
+        return (a.shape[0], *a.shape[2:]) if kind == "swap" else a.shape
+
+    blocks = [block_shape(a, kind) for a, kind in zip(arrays, kinds)]
+    slots = max(size, groups)
+
+    def body(*refs):
+        sources, targets, held = refs[:count], refs[count : 2 * count], refs[2 * count : 3 * count]
+        send, receive, load, store, up, down, arrive, across, landed = refs[3 * count :]
+        ctx, group = lax.axis_index("ctx"), lax.axis_index("fsdp")
+        place, side = ctx // 2, ctx % 2
+        position = {
+            "deal": ctx, "ctx": ctx, "chain": ctx, "fsdp": group, "line": place, "swap": side
+        }
+
+        def device(kind, j):
+            if kind == "fsdp":
+                return {"fsdp": j}
+            if kind == "line":
+                return {"ctx": j * 2 + side}
+            return {"ctx": place * 2 + j} if kind == "swap" else {"ctx": j}
+
+        def block(i, owner):
+            if kinds[i] in ("deal", "line"):
+                return sources[i].at[owner]
+            return sources[i].at[:, owner] if kinds[i] == "swap" else sources[i]
+
+        def remote(source, target, send_sem, receive_sem, device_id):
+            return pltpu.make_async_remote_copy(
+                src_ref=source,
+                dst_ref=target,
+                send_sem=send_sem,
+                recv_sem=receive_sem,
+                device_id=device_id,
+                device_id_type=pl.DeviceIdType.MESH,
+            )
+
+        own = [
+            pltpu.make_async_copy(block(i, position[kinds[i]]), held[i], load.at[i])
+            for i in range(count)
+        ]
+        for copy in own:
+            copy.start()
+        barrier = pltpu.get_barrier_semaphore()
+        greeted = [({"ctx": lax.rem(ctx + step, size)}) for step in range(1, size)]
+        if "fsdp" in kinds:
+            greeted += [{"fsdp": lax.rem(group + step, groups)} for step in range(1, groups)]
+        for peer in greeted:
+            pl.semaphore_signal(barrier, 1, device_id=peer, device_id_type=pl.DeviceIdType.MESH)
+        pl.semaphore_wait(barrier, len(greeted))
+
+        copies = []
+
+        def spread(i):
+            kind = kinds[i]
+            for step in range(1, spans[kind]):
+                peer = lax.rem(position[kind] + step, spans[kind])
+                copy = remote(
+                    block(i, peer),
+                    targets[i].at[position[kind]],
+                    send.at[i, step],
+                    receive.at[i, step],
+                    device(kind, peer),
+                )
+                copy.start()
+                copies.append(copy)
+
+        def hop(i, origin, first, ahead, sems):
+            slot = targets[i].at[origin * 2 + side]
+            source = sources[i] if first else slot
+            return remote(
+                source, slot, sems.at[origin], arrive.at[origin], {"ctx": ahead * 2 + side}
+            )
+
+        def cross(i, origin, first):
+            slot = targets[i].at[origin * 2 + side]
+            source = sources[i] if first else slot
+            return remote(
+                source, slot, across.at[origin], landed.at[origin], {"ctx": place * 2 + 1 - side}
+            )
+
+        def pass_on(i, distance, finish=False):
+            first = distance == 0
+            act = (lambda c: c.wait_send()) if finish else (lambda c: c.start())
+            for sems, sign in ((up, 1), (down, -1)):
+                origin = place - sign * distance
+                ahead = place + sign
+                there = (origin >= 0) & (origin < places)
+
+                @pl.when(there)
+                def _():
+                    if not first and not finish:
+                        hop(i, origin, first, place, sems).wait_recv()
+
+                    @pl.when((ahead >= 0) & (ahead < places))
+                    def _():
+                        act(hop(i, origin, first, ahead, sems))
+
+                    if not first or sign == 1:
+                        act(cross(i, origin, first))
+
+        chain = kinds.index("chain") if "chain" in kinds else None
+        rest = [i for i in range(count) if i != chain]
+        deals = [i for i in rest if kinds[i] == "deal"]
+        if chain is None:
+            for i in rest:
+                spread(i)
+        else:
+            pass_on(chain, 0)
+            for i in rest:
+                if i not in deals:
+                    spread(i)
+            for turn in range(max(len(deals), places - 1)):
+                if turn < len(deals):
+                    spread(deals[turn])
+                if turn < places - 1:
+                    pass_on(chain, turn + 1)
+        for i in range(count):
+            own[i].wait()
+            back = pltpu.make_async_copy(held[i], targets[i].at[position[kinds[i]]], store.at[i])
+            back.start()
+            own[i] = back
+        for copy in own + copies:
+            copy.wait()
+        if chain is not None:
+            for distance in range(places):
+                pass_on(chain, distance, finish=True)
+            for origin in range(places):
+                slot = targets[chain].at[origin * 2 + 1 - side]
+                remote(
+                    slot, slot, across.at[origin], landed.at[origin], {"ctx": place * 2 + 1 - side}
+                ).wait_recv()
+
+    return pl.pallas_call(
+        body,
+        in_specs=[pl.BlockSpec(memory_space=pl.ANY)] * count,
+        out_specs=[pl.BlockSpec(memory_space=pl.ANY)] * count,
+        out_shape=[
+            jax.ShapeDtypeStruct((spans[kind], *block), a.dtype)
+            for a, kind, block in zip(arrays, kinds, blocks)
+        ],
+        scratch_shapes=[pltpu.VMEM(block, a.dtype) for a, block in zip(arrays, blocks)]
+        + [pltpu.SemaphoreType.DMA((count, slots))] * 2
+        + [pltpu.SemaphoreType.DMA((count,))] * 2
+        + [pltpu.SemaphoreType.DMA((places,))] * 5,
+        compiler_params=pltpu.CompilerParams(collective_id=collective_id, has_side_effects=True),
+    )(*arrays)
+
+
 def per_device(query_proj, key_proj, value_proj, modality, out_weight, grad_projected):
     context_size = lax.axis_size("ctx")
     groups = lax.axis_size("fsdp")
@@ -222,36 +381,64 @@
     width = groups * piece
 
     def to_heads(flat):
-        split = flat[0].reshape(row_count, groups, context_size, piece).transpose(2, 0, 1, 3)
-        return lax.all_to_all(split, "ctx", 0, 0).reshape(length, width)
-
-    def to_rows(flat):
-        split = lax.all_to_all(
-            flat.reshape(context_size, row_count, groups, piece), "ctx", 0, 0
-        )
+        return flat[0].reshape(row_count, groups, context_size, piece).transpose(2, 0, 1, 3).reshape(
+            context_size, row_count, width
+        )
+
+    def to_rows(blocks):
+        split = blocks.reshape(context_size, row_count, groups, piece)
         return split.transpose(1, 2, 0, 3).reshape(1, row_count, width * context_size)
 
-    weight = lax.all_gather(out_weight, "fsdp", axis=1, tiled=True).reshape(2 * width, -1)
-    upstream = lax.all_gather(grad_projected[0], "ctx", axis=0, tiled=True)
-    image = (lax.all_gather(modality[0], "ctx", axis=0, tiled=True) == 1)[:, None]
-    both = transposed_product(upstream, weight)
-    grad_attention = jnp.where(image, both[:, width:], both[:, :width]).astype(jnp.bfloat16)
+    marks = jnp.broadcast_to(modality, (8, row_count))
+    weight, upstream, marks, query, key, value = exchange(
+        (
+            out_weight,
+            grad_projected[0],
+            marks,
+            to_heads(query_proj),
+            to_heads(key_proj),
+            to_heads(value_proj),
+        ),
+        ("fsdp", "chain", "ctx", "deal", "deal", "deal"),
+        0,
+    )
+    image = (marks[:, 0, :] == 1).reshape(length, 1)
+    upstream = upstream.reshape(length, -1)
+    weight = weight.reshape(groups * 2 * piece, -1)
+    both = transposed_product(upstream, weight).reshape(length, groups, 2, piece)
+    grad_attention = (
+        jnp.where(image[:, :, None], both[:, :, 1], both[:, :, 0])
+        .reshape(length, width)
+        .astype(jnp.bfloat16)
+    )
     attention, grad_q, grad_k, grad_v = fused_attention(
-        to_heads(query_proj), to_heads(key_proj), to_heads(value_proj), grad_attention
-    )
-    zero = jnp.zeros_like(attention)
-    spread = jnp.concatenate(
-        [jnp.where(image, zero, attention), jnp.where(image, attention, zero)], axis=1
-    )
+        query.reshape(length, width),
+        key.reshape(length, width),
+        value.reshape(length, width),
+        grad_attention,
+    )
+    spread = attention.reshape(length, groups, piece)
+    zero = jnp.zeros_like(spread)
+    spread = jnp.stack(
+        [jnp.where(image[:, :, None], zero, spread), jnp.where(image[:, :, None], spread, zero)],
+        axis=2,
+    ).reshape(length, 2 * width)
     partial = jnp.dot(spread, weight, preferred_element_type=jnp.float32).astype(jnp.bfloat16)
-    partial = lax.all_to_all(partial.reshape(context_size, row_count, -1), "ctx", 0, 0)
+    halves, grad_q, grad_k, grad_v = exchange(
+        [partial.reshape(context_size // 2, 2, row_count, -1)]
+        + [a.reshape(context_size, row_count, -1) for a in (grad_q, grad_k, grad_v)],
+        ("swap", "deal", "deal", "deal"),
+        1,
+    )
+    half = jnp.sum(halves.astype(jnp.float32), axis=0).astype(jnp.bfloat16)
+    (partial,) = exchange([half], ("line",), 2)
     projected = jnp.sum(partial.astype(jnp.float32), axis=0).astype(jnp.bfloat16)[None]
     return projected, to_rows(grad_q), to_rows(grad_k), to_rows(grad_v)
 
 
 def aligned(mesh, query_shape, weight_shape):
     devices = mesh.shape["fsdp"] * mesh.shape["ctx"]
-    return (weight_shape[1] // devices) % HEAD_SIZE == 0 and query_shape[1] <= 2048
+    return (weight_shape[1] // devices) % HEAD_SIZE == 0 and query_shape[1] <= 2048 and mesh.shape["ctx"] % 2 == 0
 
 
 def solution(mesh):

time: 386 us -> 312 us (0.81)
  the two profiles are of different devices: /device:TPU:0 before, /device:TPU:8 now
where the time goes in v2:
time: 312 us
  Pallas kernels  262 us (84%)
  local copies, waits for them, and re-layouts  22.8 us (7%)
  matrix products  15.8 us (5%)
  other arithmetic  10.3 us (3%)
    pallas_call x3, Pallas kernels, exchange(): pl.pallas_call(body, in_specs=[pl.BlockSpec(memory_space=pl.ANY)] * count...  244 us
    pallas_call x1, Pallas kernels, fused_attention(): pl.pallas_call(fused_attention_kernel, grid=(width // HEAD_SIZE,), in_spe...  18.3 us
    dot_general x1, matrix products, transposed_product(): lax.dot_general(left, right, (((1,), (1,)), ((), ())), preferred_element_...  7.99 us
    dot_general x1, matrix products, per_device(): jnp.dot(spread, weight, preferred_element_type=jnp.float32)  7.83 us

profile of v2, /device:TPU:8, one launch (start us, length us, event | category | flops | bytes accessed | tf_op | source)
XLA Modules:
  0.0 311.5 jit_solution(9941928999920729562)
XLA Ops:
  0.6 0.0 copy-start.4
  0.6 1.3 broadcast_in_dim.33.refs_2_
  2.0 1.4 copy.34
  3.4 0.4 copy.44
  3.8 0.0 copy-start.5
  3.9 1.2 reshape.97.refs_3_
  5.1 0.0 copy-done.4
  5.1 0.2 copy.35
  5.3 0.4 copy.43
  5.7 1.2 reshape.98.refs_4_
  7.0 0.0 copy-done.5
  7.0 0.2 copy.36
  7.2 0.4 copy.42
  7.6 1.2 reshape.99.refs_5_
  8.9 101.1 %shard_map.93 = (bf16[4,2,128,2048]{3,2,1,0:T(8,128)(2,1)}, bf16[8,128,2048]{2,1,0:T(8,128)(2,1)}, s32[8,8,128]{2,1,0:T(8,128)}, bf16[8,128,512]{2,1,0:T(8,128)(...) custom-call(bf16[2,128,2048]{2,1,0:T(8,128)(2,1)} %refs_0_.1, bf16[128,2048]{1,0:T(8,128)(2,1)} %bitcast.75, ...), custom_call_target="tpu_custom_call" | custom-call | tf_op jit(solution)/shard_map/pallas_call | solution.py:359
  110.0 0.8 compare_reduce_fusion
  110.8 8.0 %fusion.5 = bf16[1024,4,2,128]{0,3,2,1:T(8,128)(2,1)S(1)} fusion(bf16[1024,2048,1,1]{1,0,3,2:T(8,128)(2,1)} %bitcast.79, bf16[4,2,128,2048]{3,2,1,0:T(8,128)(2,1)} %get-tuple-element.23), kind=kOutput, calls=%fused_computation.13 | convolution fusion | flops 4294967296 | bytes 10485760 | tf_op jit(solution)/shard_map/dot_general | solution.py:94
  118.8 1.1 fusion.4
  119.9 0.0 copy-start.3
  119.9 0.5 copy.33
  120.5 1.5 copy.32
  122.0 1.2 select_convert_fusion.g_ref
  123.2 0.0 copy-done.3
  123.2 18.3 %shard_map.94 = (bf16[1024,512]{1,0:T(8,128)(2,1)S(1)}, bf16[1024,512]{1,0:T(8,128)(2,1)S(1)}, bf16[1024,512]{1,0:T(8,128)(2,1)S(1)}, bf16[1024,512]{1,0:T(8,128)(2,1)S(1)}) custom-call(bf16[1024,512]{1,0:T(8,128)(2,1)S(1)} %bitcast.58, bf16[1024,512]{1,0:T(8,128)(2,1)} %bitcast.80, bf16[1024,512]{1,0:T(8,128)(2,1)} %bitcast.81, ...), custom_call_target="tpu_custom_call" | custom-call | flops 4831838208 | bytes 8388608 | tf_op jit(solution)/shard_map/pallas_call | solution.py:202
  141.4 0.0 copy-start
  141.4 1.0 copy-done
  142.4 0.0 copy-start.1
  142.4 1.0 copy-done.1
  143.4 0.0 copy-start.2
  143.4 1.0 copy-done.2
  144.3 0.3 reshape.104
  144.6 0.2 broadcast_select_fusion.1
  144.9 7.8 %bitcast_convert_fusion = bf16[1024,2048]{1,0:T(8,128)(2,1)} fusion(bf16[4,2,128,2048]{3,2,1,0:T(8,128)(2,1)} %get-tuple-element.23, bf16[1024,4,1,128]{3,0,2,1:T(8,128)(2,1)S(1)} %get-tuple-element.35, bf16[1024,4,1,128]{3,0,2,1:T(8,128)(2,1)S(1)} %get-tuple-element.34), kind=kOutput, calls=%fused_computation | convolution fusion | flops 4298113024 | bytes 10485760 | tf_op jit(solution)/shard_map/dot_general | solution.py:426
  152.7 93.4 %shard_map.95 = (bf16[2,4,128,2048]{3,2,1,0:T(8,128)(2,1)}, bf16[8,128,512]{2,1,0:T(8,128)(2,1)}, bf16[8,128,512]{2,1,0:T(8,128)(2,1)}, bf16[8,128,512]{2,1,0:T(8,128)(2,1)}) custom-call(bf16[4,2,128,2048]{3,2,1,0:T(8,128)(2,1)} %bitcast.59, bf16[8,128,512]{2,1,0:T(8,128)(2,1)} %bitcast.55, bf16[8,128,512]{2,1,0:T(8,128)(2,1)} %bitcast.56, ...), custom_call_target="tpu_custom_call" | custom-call | tf_op jit(solution)/shard_map/pallas_call | solution.py:359
  246.1 5.1 %reduce_sum.24.refs_0_ = bf16[4,128,2048]{2,1,0:T(8,128)(2,1)} reduce(bf16[2,4,128,2048]{3,2,1,0:T(8,128)(2,1)} %get-tuple-element.28, bf16[]{:T(256)} %constant.6.clone.1), dimensions={0}, to_apply=%region_0.1 | reduce | flops 1048576 | bytes 6291458 | tf_op jit(solution)/shard_map/reduce_sum | solution.py:433
  251.2 0.0 copy-start.8
  251.2 48.9 %shard_map.96 = bf16[4,128,2048]{2,1,0:T(8,128)(2,1)} custom-call(bf16[4,128,2048]{2,1,0:T(8,128)(2,1)} %reduce_sum.24.refs_0_), custom_call_target="tpu_custom_call" | custom-call | tf_op jit(solution)/shard_map/pallas_call | solution.py:359
  300.2 0.0 copy-start.7
  300.2 3.0 reduce_sum.25
  303.2 0.0 copy-done.8
  303.2 0.3 reshape.109
  303.5 1.2 copy.27
  304.7 0.0 copy-start.6
  304.7 1.3 reshape.110
  306.0 0.0 copy-done.7
  306.0 0.3 reshape.111
  306.3 1.2 copy.28
  307.5 1.3 reshape.112
  308.8 0.0 copy-done.6
  308.8 0.3 reshape.113
  309.0 1.2 copy.29
  310.3 1.3 reshape.114
Async XLA Ops:
  0.6 4.5 %copy-start.4 = (bf16[1,128,4096]{2,1,0:T(8,128)(2,1)S(1)}, bf16[1,128,4096]{2,1,0:T(8,128)(2,1)}, u32[]{:S(2)}) copy-start(bf16[1,128,4096]{2,1,0:T(8,128)(2,1)} %param.7) | copy-start | bytes 3145732
  3.8 3.1 %copy-start.5 = (bf16[1,128,4096]{2,1,0:T(8,128)(2,1)S(1)}, bf16[1,128,4096]{2,1,0:T(8,128)(2,1)}, u32[]{:S(2)}) copy-start(bf16[1,128,4096]{2,1,0:T(8,128)(2,1)} %param.8) | copy-start | bytes 3145732
  119.9 3.2 %copy-start.3 = (bf16[8,128,512]{2,1,0:T(8,128)(2,1)S(1)}, bf16[8,128,512]{2,1,0:T(8,128)(2,1)}, u32[]{:S(2)}) copy-start(bf16[8,128,512]{2,1,0:T(8,128)(2,1)} %get-tuple-element.19) | copy-start | bytes 3145732
  141.4 1.0 copy-start
  142.4 1.0 copy-start.1
  143.4 1.0 copy-start.2
  251.2 52.0 %copy-start.8 = (bf16[8,128,512]{2,1,0:T(8,128)(2,1)S(1)}, bf16[8,128,512]{2,1,0:T(8,128)(2,1)}, u32[]{:S(2)}) copy-start(bf16[8,128,512]{2,1,0:T(8,128)(2,1)} %get-tuple-element.29) | copy-start | bytes 3145732
  300.2 5.8 %copy-start.7 = (bf16[8,128,512]{2,1,0:T(8,128)(2,1)S(1)}, bf16[8,128,512]{2,1,0:T(8,128)(2,1)}, u32[]{:S(2)}) copy-start(bf16[8,128,512]{2,1,0:T(8,128)(2,1)} %get-tuple-element.30) | copy-start | bytes 3145732
  304.7 4.1 %copy-start.6 = (bf16[8,128,512]{2,1,0:T(8,128)(2,1)S(1)}, bf16[8,128,512]{2,1,0:T(8,128)(2,1)}, u32[]{:S(2)}) copy-start(bf16[8,128,512]{2,1,0:T(8,128)(2,1)} %get-tuple-element.31) | copy-start | bytes 3145732
